TPU v7x, 512 devices: a whole 4x8x8 slice. The times are simulated.
512 devices in a mesh: gy: 32 (over z, x), gx: 16 (over y, core).
Axes of the slice: x: 4, y: 8, z: 8, core: 2. Of those that a mesh axis runs over, the one named last changes fastest.
Arguments:
- ensemble: float32 [64, 256, 2048], P(None, 'gy', 'gx'), may hold values from -6 to 6
- flow: float32 [3, 256, 2048], P(None, 'gy', 'gx')
- obs_cell: int32 [32, 16, 4], P('gy', 'gx'), may hold values from 0 to 1023
- obs_value: float32 [32, 16, 4], P('gy', 'gx'), may hold values from -6 to 6
- obs_var: float32 [32, 16, 4], P('gy', 'gx'), may hold values from 4 to 16
Outputs:
- analysis: float32 [64, 256, 2048], P(None, 'gy', 'gx')
All inputs are finite; a program needn't handle non-finite values.
Results may differ from a plain program's by a relative error of at most 0.0001.
Values sent between devices are 32-bit elements; how exact they have to be, the bound alone decides.
A program may use at most 64 MiB of HBM per device.

v0:
```python
import jax
import jax.numpy as jnp
from jax import lax
from jax.sharding import PartitionSpec as P


def extended(block, sides, width):
    for axis, dim in sides:
        count = lax.axis_size(axis)
        forward = [(i, i + 1) for i in range(count - 1)]
        backward = [(target, source) for source, target in forward]
        low = lax.ppermute(
            lax.slice_in_dim(block, block.shape[dim] - width, None, axis=dim), axis, forward
        )
        high = lax.ppermute(lax.slice_in_dim(block, 0, width, axis=dim), axis, backward)
        block = jnp.concatenate([low, block, high], axis=dim)
    return block


def advance(padded, coeffs):
    state_grid = padded[:, 1:-1, 1:-1]
    north = padded[:, :-2, 1:-1]
    south = padded[:, 2:, 1:-1]
    west = padded[:, 1:-1, :-2]
    east = padded[:, 1:-1, 2:]
    spread = coeffs[0] * (north + south + west + east - 4.0 * state_grid)
    return state_grid + spread - 0.5 * coeffs[1] * (east - west) - 0.5 * coeffs[2] * (south - north)


def border_update(state_grid, flow):
    padded = extended(state_grid, (("gy", 1), ("gx", 2)), 1)
    return advance(padded, flow)


def tri_solve(matrix, rhs):
    return lax.linalg.triangular_solve(matrix, rhs, left_side=True, lower=True, transpose_a=True)


def body(ensemble, flow, obs_cell, obs_value, obs_var):
    members = ensemble.shape[0]
    predicted_state = border_update(border_update(ensemble, flow), flow)
    ensemble_average = jnp.mean(predicted_state, axis=0)
    member_deviation = predicted_state - ensemble_average
    flat_anomaly = member_deviation.reshape(members, -1)
    cells = obs_cell.reshape(-1)
    factor = lax.rsqrt(obs_var.reshape(-1))
    scaled = jnp.take(flat_anomaly, cells, axis=1) * factor
    innovation = (obs_value.reshape(-1) - jnp.take(ensemble_average.reshape(-1), cells)) * factor
    eye = jnp.eye(members, dtype=jnp.float32)
    local_gram = jnp.dot(scaled, scaled.T, precision=lax.Precision.HIGHEST)
    local_target = jnp.dot(scaled, innovation, precision=lax.Precision.HIGHEST)
    gram, target = lax.psum((local_gram, local_target), ("gy", "gx"))
    lower = jnp.linalg.cholesky(gram + (members - 1.0) * eye)
    inverse = tri_solve(lower, eye)
    weights = jnp.dot(
        inverse,
        jnp.dot(inverse.T, target, precision=lax.Precision.HIGHEST),
        precision=lax.Precision.HIGHEST,
    )
    transform = jnp.sqrt(members - 1.0) * inverse + weights[:, None]
    update = jnp.dot(transform.T, flat_anomaly, precision=lax.Precision.HIGHEST)
    return ensemble_average + update.reshape(member_deviation.shape)


def solution(mesh):
    return jax.shard_map(
        body,
        mesh=mesh,
        in_specs=(
            P(None, "gy", "gx"),
            P(None, "gy", "gx"),
            P("gy", "gx", None),
            P("gy", "gx", None),
            P("gy", "gx", None),
        ),
        out_specs=P(None, "gy", "gx"),
        check_vma=False,
    )
```

profile of v0, /device:TPU:1, one launch (start us, length us, event | category | flops | bytes accessed | tf_op | source)
XLA Modules:
  0.0 169.7 jit_solution(2727058517683121358)
XLA Ops:
  0.0 0.0 copy-start
  0.0 1.1 copy.23
  1.1 0.0 copy-start.1
  1.1 3.9 %collective-permute-start = (f32[64,1,128]{2,0,1:T(8,128)S(1)}, f32[64,1,128]{2,0,1:T(8,128)S(1)}, u32[]{:S(2)}, u32[]{:S(2)}) collective-permute-start(f32[64,1,128]{2,0,1:T(8,128)S(1)} %get-tuple-element.18), channel_id=1, source_target_pairs={{0,16},{16,32},{32,48},{48,64},{64,80},{80,96},{96,112},{112,128},... | collective-permute-start | bytes 98312 | tf_op jit(solution)/shard_map/ppermute | solution.py:12
  5.1 0.0 copy-start.2
  5.1 1.3 collective-permute-start.1
  6.4 0.0 copy-done.1
  6.4 0.0 copy-done.2
  6.4 0.0 collective-permute-done
  6.4 0.0 copy-done
  6.5 3.2 %collective-permute-done.1 = f32[64,1,128]{2,0,1:T(8,128)S(1)} collective-permute-done((f32[64,1,128]{2,0,1:T(8,128)S(1)}, f32[64,1,128]{2,0,1:T(8,128)S(1)}, u32[]{:S(2)}, u32[]{:S(2)}) %collective-permute-start.1) | collective-permute-done | bytes 32800 | tf_op jit(solution)/shard_map/ppermute | solution.py:15
  9.7 0.2 fusion.34
  9.9 5.2 %collective-permute-start.2 = (f32[64,10,1]{2,0,1:T(8,128)S(1)}, f32[64,10,1]{2,0,1:T(8,128)S(1)}, u32[]{:S(2)}, u32[]{:S(2)}) collective-permute-start(f32[64,10,1]{2,0,1:T(8,128)S(1)} %get-tuple-element.11), channel_id=1, source_target_pairs={{0,1},{1,2},{2,3},{3,4},{4,5},{5,6},{6,7},{7,8},{8,9},{9,10},{10,1... | collective-permute-start | bytes 7688 | tf_op jit(solution)/shard_map/ppermute | solution.py:12
  15.1 3.4 %collective-permute-start.3 = (f32[64,10,1]{2,0,1:T(8,128)S(1)}, f32[64,10,1]{2,0,1:T(8,128)S(1)}, u32[]{:S(2)}, u32[]{:S(2)}) collective-permute-start(f32[64,10,1]{2,0,1:T(8,128)S(1)} %get-tuple-element.12), channel_id=1, source_target_pairs={{1,0},{2,1},{3,2},{4,3},{5,4},{6,5},{7,6},{8,7},{9,8},{10,9},{11,1... | collective-permute-start | bytes 7688 | tf_op jit(solution)/shard_map/ppermute | solution.py:15
  18.5 0.6 collective-permute-done.2
  19.1 4.4 %collective-permute-done.3 = f32[64,10,1]{2,0,1:T(8,128)S(1)} collective-permute-done((f32[64,10,1]{2,0,1:T(8,128)S(1)}, f32[64,10,1]{2,0,1:T(8,128)S(1)}, u32[]{:S(2)}, u32[]{:S(2)}) %collective-permute-start.3) | collective-permute-done | bytes 2592 | tf_op jit(solution)/shard_map/ppermute | solution.py:15
  23.5 0.3 multiply_subtract_fusion.1
  23.8 0.0 copy-start.3
  23.8 3.1 %collective-permute-start.4 = (f32[64,1,128]{2,0,1:T(8,128)S(1)}, f32[64,1,128]{2,0,1:T(8,128)S(1)}, u32[]{:S(2)}, u32[]{:S(2)}) collective-permute-start(f32[64,1,128]{2,0,1:T(8,128)S(1)} %get-tuple-element.15), channel_id=1, source_target_pairs={{0,16},{16,32},{32,48},{48,64},{64,80},{80,96},{96,112},{112,128},... | collective-permute-start | bytes 98312 | tf_op jit(solution)/shard_map/ppermute | solution.py:12
  26.9 1.3 collective-permute-start.5
  28.2 0.0 copy-done.3
  28.3 0.0 collective-permute-done.4
  28.3 3.3 %collective-permute-done.5 = f32[64,1,128]{2,0,1:T(8,128)S(1)} collective-permute-done((f32[64,1,128]{2,0,1:T(8,128)S(1)}, f32[64,1,128]{2,0,1:T(8,128)S(1)}, u32[]{:S(2)}, u32[]{:S(2)}) %collective-permute-start.5) | collective-permute-done | bytes 32800 | tf_op jit(solution)/shard_map/ppermute | solution.py:15
  31.6 0.2 fusion.33
  31.8 3.2 %collective-permute-start.6 = (f32[64,10,1]{2,0,1:T(8,128)S(1)}, f32[64,10,1]{2,0,1:T(8,128)S(1)}, u32[]{:S(2)}, u32[]{:S(2)}) collective-permute-start(f32[64,10,1]{2,0,1:T(8,128)S(1)} %get-tuple-element.9), channel_id=1, source_target_pairs={{0,1},{1,2},{2,3},{3,4},{4,5},{5,6},{6,7},{7,8},{8,9},{9,10},{10,1... | collective-permute-start | bytes 7688 | tf_op jit(solution)/shard_map/ppermute | solution.py:12
  35.0 1.9 %collective-permute-start.7 = (f32[64,10,1]{2,0,1:T(8,128)S(1)}, f32[64,10,1]{2,0,1:T(8,128)S(1)}, u32[]{:S(2)}, u32[]{:S(2)}) collective-permute-start(f32[64,10,1]{2,0,1:T(8,128)S(1)} %get-tuple-element.10), channel_id=1, source_target_pairs={{1,0},{2,1},{3,2},{4,3},{5,4},{6,5},{7,6},{8,7},{9,8},{10,9},{11,1... | collective-permute-start | bytes 7688 | tf_op jit(solution)/shard_map/ppermute | solution.py:15
  36.9 2.1 %collective-permute-done.6 = f32[64,10,1]{2,0,1:T(8,128)S(1)} collective-permute-done((f32[64,10,1]{2,0,1:T(8,128)S(1)}, f32[64,10,1]{2,0,1:T(8,128)S(1)}, u32[]{:S(2)}, u32[]{:S(2)}) %collective-permute-start.6) | collective-permute-done | bytes 2592 | tf_op jit(solution)/shard_map/ppermute | solution.py:12
  39.0 4.4 %collective-permute-done.7 = f32[64,10,1]{2,0,1:T(8,128)S(1)} collective-permute-done((f32[64,10,1]{2,0,1:T(8,128)S(1)}, f32[64,10,1]{2,0,1:T(8,128)S(1)}, u32[]{:S(2)}, u32[]{:S(2)}) %collective-permute-start.7) | collective-permute-done | bytes 2592 | tf_op jit(solution)/shard_map/ppermute | solution.py:15
  43.4 0.3 fusion.32
  43.7 0.2 copy.25
  43.9 0.6 gather_fusion
  44.5 0.6 gather_fusion.1
  45.1 0.0 copy-start.4
  45.1 0.3 fusion.13
  45.4 0.3 copy-done.4
  45.8 0.2 convolution_bitcast_fusion.2
  46.0 109.7 %all-reduce = (f32[64,64]{1,0:T(8,128)S(1)}, f32[64]{0:T(128)S(1)}) all-reduce(f32[64,64]{1,0:T(8,128)S(1)} %fusion.13, f32[64]{0:T(128)S(1)} %convolution_bitcast_fusion.2), channel_id=1, replica_groups=mesh['gy'=32,'gx'=16] {'gy','gx'}, use_global_device_ids=true, to_apply=%region_1.2 | all-reduce | flops 4160 | bytes 33280 | tf_op jit(solution)/shard_map/psum | solution.py:52
  155.7 0.1 copy.26
  155.8 5.8 %cholesky.17 = f32[64,64]{1,0:T(8,128)S(1)} custom-call(f32[64,64]{1,0:T(8,128)S(1)} %fusion.7), custom_call_target="Cholesky" | custom-call | tf_op jit(solution)/shard_map/jit(cholesky)/cholesky | solution.py:53
  161.6 0.6 compare_reduce_fusion
  162.3 0.7 fusion.2
  162.9 4.9 %custom-call.6 = f32[1,64,64]{1,2,0:T(8,128)S(1)} custom-call(f32[1,64,64]{2,1,0:T(8,128)S(1)} %fusion.2), custom_call_target="InvertDiagBlocksLowerTriangular" | custom-call | tf_op jit(solution)/shard_map/triangular_solve | solution.py:36
  167.8 0.2 fusion.5
  168.0 0.1 convolution_bitcast_fusion.1
  168.2 0.2 convolution_bitcast_fusion
  168.3 0.5 convolution_add_fusion
  168.8 0.9 copy.29
  (16 shorter events, 0.2 us)
Async XLA Ops:
  0.0 6.4 %copy-start = (f32[64,8,128]{2,1,0:T(8,128)S(1)}, f32[64,8,128]{2,1,0:T(8,128)}, u32[]{:S(2)}) copy-start(f32[64,8,128]{2,1,0:T(8,128)} %param.5) | copy-start | bytes 786436
  1.1 5.3 %copy-start.1 = (f32[3,8,128]{2,1,0:T(8,128)S(1)}, f32[3,8,128]{2,1,0:T(8,128)}, u32[]{:S(2)}) copy-start(f32[3,8,128]{2,1,0:T(8,128)} %param.6) | copy-start | bytes 36868
  1.1 5.3 %collective-permute-start = (f32[64,1,128]{2,0,1:T(8,128)S(1)}, f32[64,1,128]{2,0,1:T(8,128)S(1)}, u32[]{:S(2)}, u32[]{:S(2)}) collective-permute-start(f32[64,1,128]{2,0,1:T(8,128)S(1)} %get-tuple-element.18), channel_id=1, source_target_pairs={{0,16},{16,32},{32,48},{48,64},{64,80},{80,96},{96,112},{112,128},... | collective-permute-start | bytes 98312 | tf_op jit(solution)/shard_map/ppermute | solution.py:12
  5.1 1.3 copy-start.2
  5.1 4.7 %collective-permute-start.1 = (f32[64,1,128]{2,0,1:T(8,128)S(1)}, f32[64,1,128]{2,0,1:T(8,128)S(1)}, u32[]{:S(2)}, u32[]{:S(2)}) collective-permute-start(f32[64,1,128]{2,0,1:T(8,128)S(1)} %get-tuple-element.17), channel_id=1, source_target_pairs={{16,0},{32,16},{48,32},{64,48},{80,64},{96,80},{112,96},{128,112},... | collective-permute-start | bytes 98312 | tf_op jit(solution)/shard_map/ppermute | solution.py:15
  9.9 9.2 %collective-permute-start.2 = (f32[64,10,1]{2,0,1:T(8,128)S(1)}, f32[64,10,1]{2,0,1:T(8,128)S(1)}, u32[]{:S(2)}, u32[]{:S(2)}) collective-permute-start(f32[64,10,1]{2,0,1:T(8,128)S(1)} %get-tuple-element.11), channel_id=1, source_target_pairs={{0,1},{1,2},{2,3},{3,4},{4,5},{5,6},{6,7},{7,8},{8,9},{9,10},{10,1... | collective-permute-start | bytes 7688 | tf_op jit(solution)/shard_map/ppermute | solution.py:12
  15.1 8.4 %collective-permute-start.3 = (f32[64,10,1]{2,0,1:T(8,128)S(1)}, f32[64,10,1]{2,0,1:T(8,128)S(1)}, u32[]{:S(2)}, u32[]{:S(2)}) collective-permute-start(f32[64,10,1]{2,0,1:T(8,128)S(1)} %get-tuple-element.12), channel_id=1, source_target_pairs={{1,0},{2,1},{3,2},{4,3},{5,4},{6,5},{7,6},{8,7},{9,8},{10,9},{11,1... | collective-permute-start | bytes 7688 | tf_op jit(solution)/shard_map/ppermute | solution.py:15
  23.8 4.4 %copy-start.3 = (f32[1,1,4]{2,1,0:T(1,128)S(1)}, f32[1,1,4]{2,1,0:T(1,128)}, u32[]{:S(2)}) copy-start(f32[1,1,4]{2,1,0:T(1,128)} %param.9) | copy-start | bytes 52
  23.8 4.5 %collective-permute-start.4 = (f32[64,1,128]{2,0,1:T(8,128)S(1)}, f32[64,1,128]{2,0,1:T(8,128)S(1)}, u32[]{:S(2)}, u32[]{:S(2)}) collective-permute-start(f32[64,1,128]{2,0,1:T(8,128)S(1)} %get-tuple-element.15), channel_id=1, source_target_pairs={{0,16},{16,32},{32,48},{48,64},{64,80},{80,96},{96,112},{112,128},... | collective-permute-start | bytes 98312 | tf_op jit(solution)/shard_map/ppermute | solution.py:12
  26.9 4.7 %collective-permute-start.5 = (f32[64,1,128]{2,0,1:T(8,128)S(1)}, f32[64,1,128]{2,0,1:T(8,128)S(1)}, u32[]{:S(2)}, u32[]{:S(2)}) collective-permute-start(f32[64,1,128]{2,0,1:T(8,128)S(1)} %get-tuple-element.16), channel_id=1, source_target_pairs={{16,0},{32,16},{48,32},{64,48},{80,64},{96,80},{112,96},{128,112},... | collective-permute-start | bytes 98312 | tf_op jit(solution)/shard_map/ppermute | solution.py:15
  31.8 7.2 %collective-permute-start.6 = (f32[64,10,1]{2,0,1:T(8,128)S(1)}, f32[64,10,1]{2,0,1:T(8,128)S(1)}, u32[]{:S(2)}, u32[]{:S(2)}) collective-permute-start(f32[64,10,1]{2,0,1:T(8,128)S(1)} %get-tuple-element.9), channel_id=1, source_target_pairs={{0,1},{1,2},{2,3},{3,4},{4,5},{5,6},{6,7},{7,8},{8,9},{9,10},{10,1... | collective-permute-start | bytes 7688 | tf_op jit(solution)/shard_map/ppermute | solution.py:12
  35.0 8.4 %collective-permute-start.7 = (f32[64,10,1]{2,0,1:T(8,128)S(1)}, f32[64,10,1]{2,0,1:T(8,128)S(1)}, u32[]{:S(2)}, u32[]{:S(2)}) collective-permute-start(f32[64,10,1]{2,0,1:T(8,128)S(1)} %get-tuple-element.10), channel_id=1, source_target_pairs={{1,0},{2,1},{3,2},{4,3},{5,4},{6,5},{7,6},{8,7},{9,8},{10,9},{11,1... | collective-permute-start | bytes 7688 | tf_op jit(solution)/shard_map/ppermute | solution.py:15
  45.1 0.7 copy-start.4
where the time goes:
time: 170 us
  blocking collectives  110 us (65%)
  starting transfers between devices  23.3 us (14%)
  waiting for transfers between devices  18 us (11%)
  other arithmetic  12.8 us (8%)
  local copies, waits for them, and re-layouts  4.15 us (2%)
    psum x1, blocking collectives, body(): gram, target = lax.psum((local_gram, local_target), ('gy', 'gx'))  110 us
    ppermute x4, starting transfers between devices, extended(): lax.ppermute(lax.slice_in_dim(block, block.shape[dim] - width, None, axis...  15.4 us
    ppermute x4, waiting for transfers between devices, extended(): lax.ppermute(lax.slice_in_dim(block, 0, width, axis=dim), axis, backward)  15.3 us
    ppermute x4, starting transfers between devices, extended(): lax.ppermute(lax.slice_in_dim(block, 0, width, axis=dim), axis, backward)  7.9 us
    another operation x3, other arithmetic, body(): lower = jnp.linalg.cholesky(gram + (members - 1.0) * eye)  6.52 us
    another operation x2, other arithmetic, tri_solve(): lax.linalg.triangular_solve(matrix, rhs, left_side=True, lower=True, tran...  5.55 us
  transfers between devices with their start and end apart: 8, of which 6 were waited for; matrix products, arithmetic and copies ran while one was open for 0% of the time, Pallas kernels for 0%

commit v1 on v0

--- a/solution.py
+++ b/solution.py
@@ -2,6 +2,11 @@
 import jax.numpy as jnp
 from jax import lax
 from jax.sharding import PartitionSpec as P
+
+
+def match_the_shifts_all(x_in):
+    wide_out = lax.psum(x_in, "gx")
+    return lax.psum(wide_out, "gy")
 
 
 def extended(block, sides, width):
@@ -49,7 +54,7 @@
     eye = jnp.eye(members, dtype=jnp.float32)
     local_gram = jnp.dot(scaled, scaled.T, precision=lax.Precision.HIGHEST)
     local_target = jnp.dot(scaled, innovation, precision=lax.Precision.HIGHEST)
-    gram, target = lax.psum((local_gram, local_target), ("gy", "gx"))
+    gram, target = match_the_shifts_all((local_gram, local_target))
     lower = jnp.linalg.cholesky(gram + (members - 1.0) * eye)
     inverse = tri_solve(lower, eye)
     weights = jnp.dot(

time: 170 us -> 255 us (1.50)
  the two profiles are of different devices: /device:TPU:1 before, /device:TPU:288 now
where the time goes in v1:
time: 255 us
  blocking collectives  192 us (75%)
  starting transfers between devices  32.2 us (13%)
  other arithmetic  12.8 us (5%)
  waiting for transfers between devices  12.1 us (5%)
  local copies, waits for them, and re-layouts  4.15 us (2%)
    psum x1, blocking collectives, match_the_shifts_all(): return lax.psum(wide_out, 'gy')  143 us
    psum x1, blocking collectives, match_the_shifts_all(): wide_out = lax.psum(x_in, 'gx')  48.8 us
    ppermute x4, starting transfers between devices, extended(): lax.ppermute(lax.slice_in_dim(block, 0, width, axis=dim), axis, backward)  23 us
    ppermute x4, starting transfers between devices, extended(): lax.ppermute(lax.slice_in_dim(block, block.shape[dim] - width, None, axis...  9.16 us
    another operation x3, other arithmetic, body(): lower = jnp.linalg.cholesky(gram + (members - 1.0) * eye)  6.52 us
    ppermute x4, waiting for transfers between devices, extended(): lax.ppermute(lax.slice_in_dim(block, 0, width, axis=dim), axis, backward)  6.5 us
    ppermute x4, waiting for transfers between devices, extended(): lax.ppermute(lax.slice_in_dim(block, block.shape[dim] - width, None, axis...  5.61 us
    another operation x2, other arithmetic, tri_solve(): lax.linalg.triangular_solve(matrix, rhs, left_side=True, lower=True, tran...  5.55 us
  transfers between devices with their start and end apart: 8, of which 6 were waited for; matrix products, arithmetic and copies ran while one was open for 0% of the time, Pallas kernels for 0%

profile of v1, /device:TPU:288, one launch (start us, length us, event | category | flops | bytes accessed | tf_op | source)
XLA Modules:
  0.0 255.1 jit_solution(14150878703178750606)
XLA Ops:
  0.0 0.0 copy-start
  0.0 1.1 copy.23
  1.1 0.0 copy-start.1
  1.1 3.4 %collective-permute-start = (f32[64,1,128]{2,0,1:T(8,128)S(1)}, f32[64,1,128]{2,0,1:T(8,128)S(1)}, u32[]{:S(2)}, u32[]{:S(2)}) collective-permute-start(f32[64,1,128]{2,0,1:T(8,128)S(1)} %get-tuple-element.20), channel_id=1, source_target_pairs={{0,16},{16,32},{32,48},{48,64},{64,80},{80,96},{96,112},{112,128},... | collective-permute-start | bytes 98312 | tf_op jit(solution)/shard_map/ppermute | solution.py:17
  4.5 0.0 copy-start.2
  4.5 5.8 %collective-permute-start.1 = (f32[64,1,128]{2,0,1:T(8,128)S(1)}, f32[64,1,128]{2,0,1:T(8,128)S(1)}, u32[]{:S(2)}, u32[]{:S(2)}) collective-permute-start(f32[64,1,128]{2,0,1:T(8,128)S(1)} %get-tuple-element.19), channel_id=1, source_target_pairs={{16,0},{32,16},{48,32},{64,48},{80,64},{96,80},{112,96},{128,112},... | collective-permute-start | bytes 98312 | tf_op jit(solution)/shard_map/ppermute | solution.py:20
  10.3 0.0 copy-done.1
  10.3 0.0 copy-done.2
  10.3 0.0 collective-permute-done
  10.4 0.0 copy-done
  10.4 1.4 collective-permute-done.1
  11.9 0.2 fusion.34
  12.0 1.9 collective-permute-start.2
  14.0 4.9 %collective-permute-start.3 = (f32[64,10,1]{2,0,1:T(8,128)S(1)}, f32[64,10,1]{2,0,1:T(8,128)S(1)}, u32[]{:S(2)}, u32[]{:S(2)}) collective-permute-start(f32[64,10,1]{2,0,1:T(8,128)S(1)} %get-tuple-element.14), channel_id=1, source_target_pairs={{1,0},{2,1},{3,2},{4,3},{5,4},{6,5},{7,6},{8,7},{9,8},{10,9},{11,1... | collective-permute-start | bytes 7688 | tf_op jit(solution)/shard_map/ppermute | solution.py:20
  18.8 2.8 %collective-permute-done.2 = f32[64,10,1]{2,0,1:T(8,128)S(1)} collective-permute-done((f32[64,10,1]{2,0,1:T(8,128)S(1)}, f32[64,10,1]{2,0,1:T(8,128)S(1)}, u32[]{:S(2)}, u32[]{:S(2)}) %collective-permute-start.2) | collective-permute-done | bytes 2592 | tf_op jit(solution)/shard_map/ppermute | solution.py:17
  21.6 1.8 collective-permute-done.3
  23.4 0.3 multiply_subtract_fusion.1
  23.7 0.0 copy-start.3
  23.7 1.9 collective-permute-start.4
  25.6 7.5 %collective-permute-start.5 = (f32[64,1,128]{2,0,1:T(8,128)S(1)}, f32[64,1,128]{2,0,1:T(8,128)S(1)}, u32[]{:S(2)}, u32[]{:S(2)}) collective-permute-start(f32[64,1,128]{2,0,1:T(8,128)S(1)} %get-tuple-element.18), channel_id=1, source_target_pairs={{16,0},{32,16},{48,32},{64,48},{80,64},{96,80},{112,96},{128,112},... | collective-permute-start | bytes 98312 | tf_op jit(solution)/shard_map/ppermute | solution.py:20
  33.2 0.0 copy-done.3
  33.2 0.0 collective-permute-done.4
  33.2 1.5 collective-permute-done.5
  34.8 0.2 fusion.33
  35.0 1.9 collective-permute-start.6
  36.9 4.9 %collective-permute-start.7 = (f32[64,10,1]{2,0,1:T(8,128)S(1)}, f32[64,10,1]{2,0,1:T(8,128)S(1)}, u32[]{:S(2)}, u32[]{:S(2)}) collective-permute-start(f32[64,10,1]{2,0,1:T(8,128)S(1)} %get-tuple-element.12), channel_id=1, source_target_pairs={{1,0},{2,1},{3,2},{4,3},{5,4},{6,5},{7,6},{8,7},{9,8},{10,9},{11,1... | collective-permute-start | bytes 7688 | tf_op jit(solution)/shard_map/ppermute | solution.py:20
  41.8 2.8 %collective-permute-done.6 = f32[64,10,1]{2,0,1:T(8,128)S(1)} collective-permute-done((f32[64,10,1]{2,0,1:T(8,128)S(1)}, f32[64,10,1]{2,0,1:T(8,128)S(1)}, u32[]{:S(2)}, u32[]{:S(2)}) %collective-permute-start.6) | collective-permute-done | bytes 2592 | tf_op jit(solution)/shard_map/ppermute | solution.py:17
  44.6 1.8 collective-permute-done.7
  46.3 0.3 fusion.32
  46.7 0.2 copy.25
  46.9 0.6 gather_fusion
  47.4 0.6 gather_fusion.1
  48.1 0.0 copy-start.4
  48.1 0.3 fusion.13
  48.4 0.3 copy-done.4
  48.7 0.2 convolution_bitcast_fusion.2
  48.9 48.8 %all-reduce.1 = (f32[64,64]{1,0:T(8,128)S(1)}, f32[64]{0:T(128)S(1)}) all-reduce(f32[64,64]{1,0:T(8,128)S(1)} %fusion.13, f32[64]{0:T(128)S(1)} %convolution_bitcast_fusion.2), channel_id=1, replica_groups=mesh['gy'=32,'gx'=16] {'gx'}, use_global_device_ids=true, to_apply=%region_1.2 | all-reduce | flops 4160 | bytes 33280 | tf_op jit(solution)/shard_map/psum | solution.py:8
  97.7 143.3 %all-reduce = (f32[64,64]{1,0:T(8,128)S(1)}, f32[64]{0:T(128)S(1)}) all-reduce(f32[64,64]{1,0:T(8,128)S(1)} %get-tuple-element.7, f32[64]{0:T(128)S(1)} %get-tuple-element.8), channel_id=1, replica_groups=mesh['gy'=32,'gx'=16] {'gy'}, use_global_device_ids=true, to_apply=%region_2.3 | all-reduce | flops 4160 | bytes 33280 | tf_op jit(solution)/shard_map/psum | solution.py:9
  241.0 0.1 copy.26
  241.1 5.8 %cholesky.17 = f32[64,64]{1,0:T(8,128)S(1)} custom-call(f32[64,64]{1,0:T(8,128)S(1)} %fusion.7), custom_call_target="Cholesky" | custom-call | tf_op jit(solution)/shard_map/jit(cholesky)/cholesky | solution.py:58
  247.0 0.6 compare_reduce_fusion
  247.7 0.7 fusion.2
  248.3 4.9 %custom-call.6 = f32[1,64,64]{1,2,0:T(8,128)S(1)} custom-call(f32[1,64,64]{2,1,0:T(8,128)S(1)} %fusion.2), custom_call_target="InvertDiagBlocksLowerTriangular" | custom-call | tf_op jit(solution)/shard_map/triangular_solve | solution.py:41
  253.2 0.2 fusion.5
  253.4 0.1 convolution_bitcast_fusion.1
  253.5 0.2 convolution_bitcast_fusion
  253.7 0.5 convolution_add_fusion
  254.2 0.9 copy.29
  (16 shorter events, 0.2 us)
Async XLA Ops:
  0.0 10.4 %copy-start = (f32[64,8,128]{2,1,0:T(8,128)S(1)}, f32[64,8,128]{2,1,0:T(8,128)}, u32[]{:S(2)}) copy-start(f32[64,8,128]{2,1,0:T(8,128)} %param.5) | copy-start | bytes 786436
  1.1 9.2 %copy-start.1 = (f32[3,8,128]{2,1,0:T(8,128)S(1)}, f32[3,8,128]{2,1,0:T(8,128)}, u32[]{:S(2)}) copy-start(f32[3,8,128]{2,1,0:T(8,128)} %param.6) | copy-start | bytes 36868
  1.1 9.2 %collective-permute-start = (f32[64,1,128]{2,0,1:T(8,128)S(1)}, f32[64,1,128]{2,0,1:T(8,128)S(1)}, u32[]{:S(2)}, u32[]{:S(2)}) collective-permute-start(f32[64,1,128]{2,0,1:T(8,128)S(1)} %get-tuple-element.20), channel_id=1, source_target_pairs={{0,16},{16,32},{32,48},{48,64},{64,80},{80,96},{96,112},{112,128},... | collective-permute-start | bytes 98312 | tf_op jit(solution)/shard_map/ppermute | solution.py:17
  4.5 5.8 %copy-start.2 = (s32[1,1,4]{2,1,0:T(1,128)S(1)}, s32[1,1,4]{2,1,0:T(1,128)}, u32[]{:S(2)}) copy-start(s32[1,1,4]{2,1,0:T(1,128)} %param.7) | copy-start | bytes 52
  4.5 7.3 %collective-permute-start.1 = (f32[64,1,128]{2,0,1:T(8,128)S(1)}, f32[64,1,128]{2,0,1:T(8,128)S(1)}, u32[]{:S(2)}, u32[]{:S(2)}) collective-permute-start(f32[64,1,128]{2,0,1:T(8,128)S(1)} %get-tuple-element.19), channel_id=1, source_target_pairs={{16,0},{32,16},{48,32},{64,48},{80,64},{96,80},{112,96},{128,112},... | collective-permute-start | bytes 98312 | tf_op jit(solution)/shard_map/ppermute | solution.py:20
  12.0 9.6 %collective-permute-start.2 = (f32[64,10,1]{2,0,1:T(8,128)S(1)}, f32[64,10,1]{2,0,1:T(8,128)S(1)}, u32[]{:S(2)}, u32[]{:S(2)}) collective-permute-start(f32[64,10,1]{2,0,1:T(8,128)S(1)} %get-tuple-element.13), channel_id=1, source_target_pairs={{0,1},{1,2},{2,3},{3,4},{4,5},{5,6},{6,7},{7,8},{8,9},{9,10},{10,1... | collective-permute-start | bytes 7688 | tf_op jit(solution)/shard_map/ppermute | solution.py:17
  14.0 9.4 %collective-permute-start.3 = (f32[64,10,1]{2,0,1:T(8,128)S(1)}, f32[64,10,1]{2,0,1:T(8,128)S(1)}, u32[]{:S(2)}, u32[]{:S(2)}) collective-permute-start(f32[64,10,1]{2,0,1:T(8,128)S(1)} %get-tuple-element.14), channel_id=1, source_target_pairs={{1,0},{2,1},{3,2},{4,3},{5,4},{6,5},{7,6},{8,7},{9,8},{10,9},{11,1... | collective-permute-start | bytes 7688 | tf_op jit(solution)/shard_map/ppermute | solution.py:20
  23.7 9.5 %copy-start.3 = (f32[1,1,4]{2,1,0:T(1,128)S(1)}, f32[1,1,4]{2,1,0:T(1,128)}, u32[]{:S(2)}) copy-start(f32[1,1,4]{2,1,0:T(1,128)} %param.9) | copy-start | bytes 52
  23.7 9.5 %collective-permute-start.4 = (f32[64,1,128]{2,0,1:T(8,128)S(1)}, f32[64,1,128]{2,0,1:T(8,128)S(1)}, u32[]{:S(2)}, u32[]{:S(2)}) collective-permute-start(f32[64,1,128]{2,0,1:T(8,128)S(1)} %get-tuple-element.17), channel_id=1, source_target_pairs={{0,16},{16,32},{32,48},{48,64},{64,80},{80,96},{96,112},{112,128},... | collective-permute-start | bytes 98312 | tf_op jit(solution)/shard_map/ppermute | solution.py:17
  25.6 9.1 %collective-permute-start.5 = (f32[64,1,128]{2,0,1:T(8,128)S(1)}, f32[64,1,128]{2,0,1:T(8,128)S(1)}, u32[]{:S(2)}, u32[]{:S(2)}) collective-permute-start(f32[64,1,128]{2,0,1:T(8,128)S(1)} %get-tuple-element.18), channel_id=1, source_target_pairs={{16,0},{32,16},{48,32},{64,48},{80,64},{96,80},{112,96},{128,112},... | collective-permute-start | bytes 98312 | tf_op jit(solution)/shard_map/ppermute | solution.py:20
  35.0 9.6 %collective-permute-start.6 = (f32[64,10,1]{2,0,1:T(8,128)S(1)}, f32[64,10,1]{2,0,1:T(8,128)S(1)}, u32[]{:S(2)}, u32[]{:S(2)}) collective-permute-start(f32[64,10,1]{2,0,1:T(8,128)S(1)} %get-tuple-element.11), channel_id=1, source_target_pairs={{0,1},{1,2},{2,3},{3,4},{4,5},{5,6},{6,7},{7,8},{8,9},{9,10},{10,1... | collective-permute-start | bytes 7688 | tf_op jit(solution)/shard_map/ppermute | solution.py:17
  36.9 9.4 %collective-permute-start.7 = (f32[64,10,1]{2,0,1:T(8,128)S(1)}, f32[64,10,1]{2,0,1:T(8,128)S(1)}, u32[]{:S(2)}, u32[]{:S(2)}) collective-permute-start(f32[64,10,1]{2,0,1:T(8,128)S(1)} %get-tuple-element.12), channel_id=1, source_target_pairs={{1,0},{2,1},{3,2},{4,3},{5,4},{6,5},{7,6},{8,7},{9,8},{10,9},{11,1... | collective-permute-start | bytes 7688 | tf_op jit(solution)/shard_map/ppermute | solution.py:20
  48.1 0.7 copy-start.4
